TPU v7x, 128 devices: a whole 4x4x4 slice. The times are simulated.
128 devices in a mesh: ctx: 16 (over x_lo, z, core), head: 8 (over x_hi, y).
Axes of the slice: x: 4 (x_hi: 2, x_lo: 2; x = x_hi * 2 + x_lo), y: 4, z: 4, core: 2. Of those that a mesh axis runs over, the one named last changes fastest.
Arguments:
- queries: bfloat16 [4096, 4096], P(('ctx', 'head')), may hold values from -10 to 10
- keys: bfloat16 [4096, 4096], P(('ctx', 'head')), may hold values from -10 to 10
- values: bfloat16 [4096, 4096], P(('ctx', 'head')), may hold values from -6 to 6
- grad_out: bfloat16 [4096, 4096], P(('ctx', 'head')), may hold values from -6 to 6
- block_doc: int32 [32], replicated, may hold values from 0 to 7, as said below
Outputs:
- attn_out: bfloat16 [4096, 4096], P(('ctx', 'head'))
- d_q: bfloat16 [4096, 4096], P(('ctx', 'head'))
- d_k: bfloat16 [4096, 4096], P(('ctx', 'head'))
- d_v: bfloat16 [4096, 4096], P(('ctx', 'head'))
Inputs may be any that keep to these rules, and one draw needn't show every extreme that they name: `block_doc`: document numbers never fall; every document covers at least one block; the last document covers exactly 16 blocks and every other one fewer.
All inputs are finite; a program needn't handle non-finite values.
Results may differ from a plain program's by a relative error of at most 0.03.
Values may be sent and summed in bfloat16 or wider, within the bound.
No kernel may reach another device: no remote copies, remote signals or barrier semaphores. Data moves between devices by JAX's collectives and lax.ppermute only.
A program may use at most 128 MiB of HBM per device.

v0:
```python
import math
import jax
import jax.numpy as jnp
from jax import lax
from jax.sharding import PartitionSpec as P

HD = 128
BLK = 128
masked_low = -1e30


def document_of(block_doc, positions):
    hits = positions[:, None] // BLK == lax.iota(jnp.int32, block_doc.shape[0])[None, :]
    return jnp.sum(jnp.where(hits, block_doc[None, :], 0), axis=1)


def token_positions(first_row, count, row_count, cycle_size):
    rows = first_row + lax.iota(jnp.int32, count)
    owner = rows // row_count
    local = rows % row_count
    half = row_count // 2
    return jnp.where(
        local < half, owner * half + local, (2 * cycle_size - 1 - owner) * half + local - half
    )


def visible(block_doc, query_pos, key_pos):
    same_doc = (
        document_of(block_doc, query_pos)[:, None] == document_of(block_doc, key_pos)[None, :]
    )
    return same_doc & (key_pos[None, :] <= query_pos[:, None])


def forward_update(running, query_heads, key_part, value_part, live, score_scale):
    accum, run_max, run_sum = running
    scores = (
        jnp.einsum("qhd,khd->hqk", query_heads, key_part, preferred_element_type=jnp.float32)
        * score_scale
    )
    scores = jnp.where(live[None], scores, masked_low)
    new_max = jnp.maximum(run_max, jnp.max(scores, axis=2))
    shifted = jnp.where(live[None], jnp.exp(scores - new_max[:, :, None]), 0.0)
    fading = jnp.exp(run_max - new_max)
    new_sum = run_sum * fading + jnp.sum(shifted, axis=2)
    product = jnp.einsum(
        "hqk,khd->qhd", shifted.astype(jnp.bfloat16), value_part, preferred_element_type=jnp.float32
    )
    return (accum * fading.T[:, :, None] + product, new_max, new_sum)


def backward_tile(saved, key_part, value_part, live, score_scale):
    query_heads, grad_heads, log_total, delta = saved
    scores = (
        jnp.einsum("qhd,khd->hqk", query_heads, key_part, preferred_element_type=jnp.float32)
        * score_scale
    )
    probs = jnp.where(live[None], jnp.exp(scores - log_total[:, :, None]), 0.0)
    back_weights = probs.astype(jnp.bfloat16)
    grad_value = jnp.einsum(
        "hqk,qhd->khd", back_weights, grad_heads, preferred_element_type=jnp.float32
    )
    grad_weights = jnp.einsum(
        "qhd,khd->hqk", grad_heads, value_part, preferred_element_type=jnp.float32
    )
    grad_scores = (probs * (grad_weights - delta[:, :, None])).astype(jnp.bfloat16)
    grad_query = (
        jnp.einsum("hqk,khd->qhd", grad_scores, key_part, preferred_element_type=jnp.float32)
        * score_scale
    )
    grad_key = (
        jnp.einsum("hqk,qhd->khd", grad_scores, query_heads, preferred_element_type=jnp.float32)
        * score_scale
    )
    return (grad_query, grad_key, grad_value)


def per_device(queries, keys, values, grad_out, block_doc):
    query_here, key_here, value_here, grad_here = (
        lax.all_to_all(queries, "head", split_axis=1, concat_axis=0, tiled=True),
        lax.all_to_all(keys, "head", split_axis=1, concat_axis=0, tiled=True),
        lax.all_to_all(values, "head", split_axis=1, concat_axis=0, tiled=True),
        lax.all_to_all(grad_out, "head", split_axis=1, concat_axis=0, tiled=True),
    )
    row_count = query_here.shape[0]
    feature_width = query_here.shape[1]
    local_heads = feature_width // HD
    score_scale = HD ** (-0.5)
    cycle_size = lax.axis_size("ctx")
    position = lax.axis_index("ctx")
    query_pos = token_positions(position * row_count, row_count, row_count, cycle_size)
    query_heads = query_here.reshape(row_count, local_heads, HD)
    grad_heads = grad_here.reshape(row_count, local_heads, HD)

    def fold_keys(running, pieces, first_row):
        key_part = pieces[0].reshape(-1, local_heads, HD)
        value_part = pieces[1].reshape(-1, local_heads, HD)
        key_pos = token_positions(first_row, key_part.shape[0], row_count, cycle_size)
        live = visible(block_doc, query_pos, key_pos)
        return forward_update(running, query_heads, key_part, value_part, live, score_scale)

    start_fold = (
        jnp.zeros((row_count, local_heads, HD), jnp.float32),
        jnp.full((local_heads, row_count), masked_low, jnp.float32),
        jnp.zeros((local_heads, row_count), jnp.float32),
    )
    gathered = lax.all_gather(jnp.stack((key_here, value_here)), "ctx", axis=1, tiled=True)
    span = row_count * math.gcd(cycle_size, max(1, 512 // row_count))
    block_total = cycle_size * row_count // span

    def forward_block(block_index, running):
        first_row = block_index * span
        part = lax.dynamic_slice_in_dim(gathered, first_row, span, 1)
        return fold_keys(running, (part[0], part[1]), first_row)

    accum, run_max, run_sum = lax.fori_loop(0, block_total, forward_block, start_fold)
    out_heads = (accum / run_sum.T[:, :, None]).astype(jnp.bfloat16)
    log_total = run_max + jnp.log(run_sum)
    delta = jnp.sum(grad_heads.astype(jnp.float32) * out_heads.astype(jnp.float32), axis=2).T
    saved = (query_heads, grad_heads, log_total, delta)

    def tile_grads(key_flat, value_flat, key_start):
        key_part = key_flat.reshape(-1, local_heads, HD)
        value_part = value_flat.reshape(-1, local_heads, HD)
        key_pos = token_positions(key_start, key_part.shape[0], row_count, cycle_size)
        live = visible(block_doc, query_pos, key_pos)
        return backward_tile(saved, key_part, value_part, live, score_scale)

    def backward_block(block_index, state):
        grad_query, key_sums = state
        first_row = block_index * span
        part = lax.dynamic_slice_in_dim(gathered, first_row, span, 1)
        add_query, add_key, add_value = tile_grads(part[0], part[1], first_row)
        key_sums = lax.dynamic_update_slice_in_dim(
            key_sums, jnp.stack((add_key, add_value)), first_row, 1
        )
        return (grad_query + add_query, key_sums)

    start_back = (
        jnp.zeros((row_count, local_heads, HD), jnp.float32),
        jnp.zeros((2, cycle_size * row_count, local_heads, HD), jnp.float32),
    )
    grad_query, key_sums = lax.fori_loop(0, block_total, backward_block, start_back)
    grad_key, grad_value = (
        lax.psum_scatter(
            key_sums[0].astype(jnp.bfloat16), "ctx", scatter_dimension=0, tiled=True
        ).astype(jnp.float32),
        lax.psum_scatter(
            key_sums[1].astype(jnp.bfloat16), "ctx", scatter_dimension=0, tiled=True
        ).astype(jnp.float32),
    )
    out_flat = out_heads.reshape(row_count, feature_width)
    query_flat = grad_query.astype(jnp.bfloat16).reshape(row_count, feature_width)
    key_flat = grad_key.astype(jnp.bfloat16).reshape(row_count, feature_width)
    value_flat = grad_value.astype(jnp.bfloat16).reshape(row_count, feature_width)
    return (
        lax.all_to_all(out_flat, "head", split_axis=0, concat_axis=1, tiled=True),
        lax.all_to_all(query_flat, "head", split_axis=0, concat_axis=1, tiled=True),
        lax.all_to_all(key_flat, "head", split_axis=0, concat_axis=1, tiled=True),
        lax.all_to_all(value_flat, "head", split_axis=0, concat_axis=1, tiled=True),
    )


def solution(mesh):
    return jax.shard_map(
        per_device,
        mesh=mesh,
        in_specs=(
            P(("ctx", "head"), None),
            P(("ctx", "head"), None),
            P(("ctx", "head"), None),
            P(("ctx", "head"), None),
            P(),
        ),
        out_specs=(
            P(("ctx", "head"), None),
            P(("ctx", "head"), None),
            P(("ctx", "head"), None),
            P(("ctx", "head"), None),
        ),
        check_vma=False,
    )
```

profile of v0, /device:TPU:0, one launch (start us, length us, event | category | flops | bytes accessed | tf_op | source)
XLA Modules:
  0.0 350.0 jit_solution(4947090339236871843)
XLA Ops:
  7.2 1.7 copy.146
  8.9 7.2 %all-to-all-start = ((bf16[32,8,512]{2,0,1:T(8,128)(2,1)}), bf16[32,8,512]{2,0,1:T(8,128)(2,1)S(1)}, u32[]{:S(2)}, u32[]{:S(2)}) async-start(bf16[32,8,512]{2,0,1:T(8,128)(2,1)} %bitcast.94), calls=%async_computation | async-start | bytes 524288 | tf_op jit(solution)/shard_map/all_to_all | solution.py:80
  17.1 7.7 %all-to-all-done = bf16[32,8,512]{2,0,1:T(8,128)(2,1)S(1)} async-done(((bf16[32,8,512]{2,0,1:T(8,128)(2,1)}), bf16[32,8,512]{2,0,1:T(8,128)(2,1)S(1)}, u32[]{:S(2)}, u32[]{:S(2)}) %all-to-all-start) | async-done | bytes 262176 | tf_op jit(solution)/shard_map/all_to_all | solution.py:80
  24.8 11.3 %all_to_all.140 = bf16[32,8,512]{2,0,1:T(8,128)(2,1)S(1)} all-to-all(bf16[32,8,512]{2,0,1:T(8,128)(2,1)S(1)} %bitcast.162), channel_id=1, replica_groups=mesh['ctx'=16,'head'=8] {'head'}, dimensions={1} | all-to-all | bytes 524288 | tf_op jit(solution)/shard_map/all_to_all | solution.py:81
  37.7 3.4 all-to-all-start.2
  41.9 7.9 %all-to-all-done.2 = bf16[32,8,512]{2,0,1:T(8,128)(2,1)S(1)} async-done(((bf16[32,8,512]{2,0,1:T(8,128)(2,1)}), bf16[32,8,512]{2,0,1:T(8,128)(2,1)S(1)}, u32[]{:S(2)}, u32[]{:S(2)}) %all-to-all-start.2) | async-done | bytes 262176 | tf_op jit(solution)/shard_map/all_to_all | solution.py:79
  49.8 3.4 all-to-all-start.4
  53.4 10.4 %all-to-all-done.4 = bf16[32,8,512]{2,0,1:T(8,128)(2,1)S(1)} async-done(((bf16[32,8,512]{2,0,1:T(8,128)(2,1)}), bf16[32,8,512]{2,0,1:T(8,128)(2,1)S(1)}, u32[]{:S(2)}, u32[]{:S(2)}) %all-to-all-start.4) | async-done | bytes 262176 | tf_op jit(solution)/shard_map/all_to_all | solution.py:82
  63.9 26.2 %all-gather.2.cloned.1.call-done = bf16[2,4096,512]{2,1,0:T(8,128)(2,1)} async-done(((bf16[2,256,512]{2,1,0:T(8,128)(2,1)}), bf16[2,4096,512]{2,1,0:T(8,128)(2,1)}) %all-gather.2.cloned.1.call-update) | async-done | bytes 8388624 | tf_op jit(solution)/shard_map/all_gather | solution.py:106
  90.1 11.3 %copy.110 = bf16[2,4096,512]{1,2,0:T(8,128)(2,1)} copy(bf16[2,4096,512]{2,1,0:T(8,128)(2,1)} %all-gather.2.cloned.1.call-done) | data formatting | bytes 16777216
  101.5 29.7 %while.44 = (s32[]{:T(128)}, f32[256,4,128]{0,2,1:T(8,128)S(1)}, f32[4,256]{1,0:T(4,128)S(1)}, f32[4,256]{1,0:T(4,128)S(1)}, s32[32]{0:T(128)S(1)}, /*index=5*/b...) while((s32[]{:T(128)}, f32[256,4,128]{0,2,1:T(8,128)S(1)}, ...), condition=%wide.region_5.6_spmd.clone.clone.clone, body=%wide.region_0.5_spmd.clone.clone.clone.sunk | while | flops 276164096 | bytes 11359203 | solution.py:115
  102.0 1.3 constant_dynamic-slice_fusion.6
  105.7 1.3 constant_dynamic-slice_fusion.6
  109.4 1.3 constant_dynamic-slice_fusion.6
  113.1 1.3 constant_dynamic-slice_fusion.6
  116.8 1.3 constant_dynamic-slice_fusion.6
  120.5 1.3 constant_dynamic-slice_fusion.6
  124.2 1.3 constant_dynamic-slice_fusion.6
  128.0 1.3 constant_dynamic-slice_fusion.6
  132.3 4.3 %broadcast_in_dim.271 = bf16[2,4096,4,128]{3,1,2,0:T(8,128)(2,1)} broadcast(bf16[]{:T(256)} %constant.563), dimensions={} | broadcast | bytes 8388610 | tf_op jit(solution)/shard_map/broadcast_in_dim | solution.py:140
  136.6 43.1 %while.45 = (s32[]{:T(128)}, f32[256,4,128]{0,2,1:T(8,128)S(1)}, bf16[2,4096,4,128]{3,1,2,0:T(8,128)(2,1)}, bf16[2,4096,512]{1,2,0:T(8,128)(2,1)}, s32[32]{0:T(1...) while((s32[]{:T(128)}, f32[256,4,128]{0,2,1:T(8,128)S(1)}, ...), condition=%wide.region_10.11_spmd.clone.clone.clone, body=%wide.region_7.10_spmd.clone.clone.clone.sunk | while | flops 678286848 | bytes 18641908 | solution.py:142
  137.1 1.3 constant_dynamic-slice_fusion.7
  140.8 1.1 maximum_dynamic-update-slice_fusion.2
  142.5 1.3 constant_dynamic-slice_fusion.7
  146.2 1.1 maximum_dynamic-update-slice_fusion.2
  147.8 1.3 constant_dynamic-slice_fusion.7
  151.6 1.2 maximum_dynamic-update-slice_fusion.2
  153.2 1.3 constant_dynamic-slice_fusion.7
  157.0 1.1 maximum_dynamic-update-slice_fusion.2
  158.6 1.3 constant_dynamic-slice_fusion.7
  162.3 1.2 maximum_dynamic-update-slice_fusion.2
  164.0 1.3 constant_dynamic-slice_fusion.7
  167.7 1.2 maximum_dynamic-update-slice_fusion.2
  169.4 1.3 constant_dynamic-slice_fusion.7
  173.1 1.2 maximum_dynamic-update-slice_fusion.2
  174.8 1.3 constant_dynamic-slice_fusion.7
  178.6 1.1 maximum_dynamic-update-slice_fusion.2
  179.7 5.7 %slice_bitcast_fusion = (bf16[4096,4,128]{2,0,1:T(8,128)(2,1)}, bf16[4096,4,128]{2,0,1:T(8,128)(2,1)}) fusion(bf16[2,4096,4,128]{3,1,2,0:T(8,128)(2,1)} %get-tuple-element.567), kind=kLoop, calls=%fused_computation.121 | loop fusion | bytes 16777216 | tf_op jit(solution)/shard_map/convert_element_type | solution.py:148
  187.0 6.4 %all-to-all-start.3 = ((bf16[8,32,512]{2,1,0:T(8,128)(2,1)}), bf16[8,32,512]{2,1,0:T(8,128)(2,1)S(1)}, u32[]{:S(2)}, u32[]{:S(2)}) async-start(bf16[8,32,512]{2,1,0:T(8,128)(2,1)} %all_to_all.113), calls=%async_computation.3 | async-start | bytes 524288 | tf_op jit(solution)/shard_map/all_to_all | solution.py:156
  194.4 8.1 %all-to-all-done.3 = bf16[8,32,512]{2,1,0:T(8,128)(2,1)S(1)} async-done(((bf16[8,32,512]{2,1,0:T(8,128)(2,1)}), bf16[8,32,512]{2,1,0:T(8,128)(2,1)S(1)}, u32[]{:S(2)}, u32[]{:S(2)}) %all-to-all-start.3) | async-done | bytes 262176 | tf_op jit(solution)/shard_map/all_to_all | solution.py:156
  202.5 3.4 all-to-all-start.5
  205.9 50.0 %reduce-scatter.3.cloned.1.call-done = bf16[256,4,128]{2,0,1:T(8,128)(2,1)} async-done(((bf16[4096,4,128]{2,0,1:T(8,128)(2,1)}), bf16[256,4,128]{2,0,1:T(8,128)(2,1)}) %reduce-scatter.3.cloned.1.call-update) | async-done | bytes 262160 | tf_op jit(solution)/shard_map/reduce_scatter | solution.py:144
  255.9 1.2 copy.122
  257.8 7.6 %all-to-all-start.6 = ((bf16[8,32,512]{2,1,0:T(8,128)(2,1)}), bf16[8,32,512]{2,1,0:T(8,128)(2,1)S(1)}, u32[]{:S(2)}, u32[]{:S(2)}) async-start(bf16[8,32,512]{2,1,0:T(8,128)(2,1)} %all_to_all.124), calls=%async_computation.7 | async-start | bytes 524288 | tf_op jit(solution)/shard_map/all_to_all | solution.py:158
  265.5 60.2 %reduce-scatter.5.cloned.1.call-done = bf16[256,4,128]{2,0,1:T(8,128)(2,1)} async-done(((bf16[4096,4,128]{2,0,1:T(8,128)(2,1)}), bf16[256,4,128]{2,0,1:T(8,128)(2,1)}) %reduce-scatter.5.cloned.1.call-update) | async-done | bytes 262160 | tf_op jit(solution)/shard_map/reduce_scatter | solution.py:147
  325.6 1.2 copy.124
  327.6 6.4 %all-to-all-start.7 = ((bf16[8,32,512]{2,1,0:T(8,128)(2,1)}), bf16[8,32,512]{2,1,0:T(8,128)(2,1)S(1)}, u32[]{:S(2)}, u32[]{:S(2)}) async-start(bf16[8,32,512]{2,1,0:T(8,128)(2,1)} %all_to_all.128), calls=%async_computation.9 | async-start | bytes 524288 | tf_op jit(solution)/shard_map/all_to_all | solution.py:159
  336.2 6.6 %all-to-all-done.7 = bf16[8,32,512]{2,1,0:T(8,128)(2,1)S(1)} async-done(((bf16[8,32,512]{2,1,0:T(8,128)(2,1)}), bf16[8,32,512]{2,1,0:T(8,128)(2,1)S(1)}, u32[]{:S(2)}, u32[]{:S(2)}) %all-to-all-start.7) | async-done | bytes 262176 | tf_op jit(solution)/shard_map/all_to_all | solution.py:159
  (241 shorter events, 53.9 us)
Async XLA Ops:
  7.2 29.8 %copy-start = (bf16[32,4096]{1,0:T(8,128)(2,1)S(1)}, bf16[32,4096]{1,0:T(8,128)(2,1)}, u32[]{:S(2)}) copy-start(bf16[32,4096]{1,0:T(8,128)(2,1)} %param.9) | copy-start | bytes 786436
  8.9 32.2 %copy-start.1 = (bf16[32,4096]{1,0:T(8,128)(2,1)S(1)}, bf16[32,4096]{1,0:T(8,128)(2,1)}, u32[]{:S(2)}) copy-start(bf16[32,4096]{1,0:T(8,128)(2,1)} %param.12) | copy-start | bytes 786436
  8.9 15.9 %all-to-all-start = ((bf16[32,8,512]{2,0,1:T(8,128)(2,1)}), bf16[32,8,512]{2,0,1:T(8,128)(2,1)S(1)}, u32[]{:S(2)}, u32[]{:S(2)}) async-start(bf16[32,8,512]{2,0,1:T(8,128)(2,1)} %bitcast.94), calls=%async_computation | async-start | bytes 524288 | tf_op jit(solution)/shard_map/all_to_all | solution.py:80
  16.1 74.0 %all-gather.2.cloned.1.call-start = ((), (), s32[]{:S(2)}) async-start(), calls=%async_computation.10 | async-start | bytes 8912896 | tf_op jit(solution)/shard_map/all_gather | solution.py:106
  37.7 12.1 %all-to-all-start.2 = ((bf16[32,8,512]{2,0,1:T(8,128)(2,1)}), bf16[32,8,512]{2,0,1:T(8,128)(2,1)S(1)}, u32[]{:S(2)}, u32[]{:S(2)}) async-start(bf16[32,8,512]{2,0,1:T(8,128)(2,1)} %bitcast.92), calls=%async_computation.2 | async-start | bytes 524288 | tf_op jit(solution)/shard_map/all_to_all | solution.py:79
  49.8 14.0 %all-to-all-start.4 = ((bf16[32,8,512]{2,0,1:T(8,128)(2,1)}), bf16[32,8,512]{2,0,1:T(8,128)(2,1)S(1)}, u32[]{:S(2)}, u32[]{:S(2)}) async-start(bf16[32,8,512]{2,0,1:T(8,128)(2,1)} %bitcast.91), calls=%async_computation.4 | async-start | bytes 524288 | tf_op jit(solution)/shard_map/all_to_all | solution.py:82
  53.2 202.7 %reduce-scatter.3.cloned.1.call-start = ((), (), s32[]{:S(2)}) async-start(), calls=%async_computation.11 | async-start | bytes 4456448 | tf_op jit(solution)/shard_map/reduce_scatter | solution.py:144
  63.9 37.5 %copy-start.2 = (s32[32]{0:T(128)S(1)}, s32[32]{0:T(128)}, u32[]{:S(2)}) copy-start(s32[32]{0:T(128)} %param.13) | copy-start | bytes 388
  185.4 140.2 %reduce-scatter.5.cloned.1.call-start = ((), (), s32[]{:S(2)}) async-start(), calls=%async_computation.12 | async-start | bytes 4456448 | tf_op jit(solution)/shard_map/reduce_scatter | solution.py:147
  187.0 15.5 %all-to-all-start.3 = ((bf16[8,32,512]{2,1,0:T(8,128)(2,1)}), bf16[8,32,512]{2,1,0:T(8,128)(2,1)S(1)}, u32[]{:S(2)}, u32[]{:S(2)}) async-start(bf16[8,32,512]{2,1,0:T(8,128)(2,1)} %all_to_all.113), calls=%async_computation.3 | async-start | bytes 524288 | tf_op jit(solution)/shard_map/all_to_all | solution.py:156
  202.5 55.3 %all-to-all-start.5 = ((bf16[8,32,512]{2,1,0:T(8,128)(2,1)}), bf16[8,32,512]{2,1,0:T(8,128)(2,1)S(1)}, u32[]{:S(2)}, u32[]{:S(2)}) async-start(bf16[8,32,512]{2,1,0:T(8,128)(2,1)} %all_to_all.120), calls=%async_computation.5 | async-start | bytes 524288 | tf_op jit(solution)/shard_map/all_to_all | solution.py:157
  257.8 69.8 %all-to-all-start.6 = ((bf16[8,32,512]{2,1,0:T(8,128)(2,1)}), bf16[8,32,512]{2,1,0:T(8,128)(2,1)S(1)}, u32[]{:S(2)}, u32[]{:S(2)}) async-start(bf16[8,32,512]{2,1,0:T(8,128)(2,1)} %all_to_all.124), calls=%async_computation.7 | async-start | bytes 524288 | tf_op jit(solution)/shard_map/all_to_all | solution.py:158
  327.6 15.1 %all-to-all-start.7 = ((bf16[8,32,512]{2,1,0:T(8,128)(2,1)}), bf16[8,32,512]{2,1,0:T(8,128)(2,1)S(1)}, u32[]{:S(2)}, u32[]{:S(2)}) async-start(bf16[8,32,512]{2,1,0:T(8,128)(2,1)} %all_to_all.128), calls=%async_computation.9 | async-start | bytes 524288 | tf_op jit(solution)/shard_map/all_to_all | solution.py:159
Sparse Core Ops, SparseCore 0:
  37.1 52.9 all-gather.1
  185.6 70.2 reduce-scatter.2
  258.3 67.2 reduce-scatter.4
where the time goes:
time: 352 us; the launch traced here: 350 us
  waiting for transfers between devices  178 us (51%)
  local copies, waits for them, and re-layouts  55.3 us (16%)
  starting transfers between devices  38 us (11%)
  matrix products  29.8 us (8%)
  other arithmetic  23 us (7%)
  between operations  13.9 us (4%)
  blocking collectives  11.3 us (3%)
    reduce_scatter x1, waiting for transfers between devices, per_device(): lax.psum_scatter(key_sums[1].astype(jnp.bfloat16), 'ctx', scatter_dimensi...  60.2 us
    reduce_scatter x1, waiting for transfers between devices, per_device(): lax.psum_scatter(key_sums[0].astype(jnp.bfloat16), 'ctx', scatter_dimensi...  50 us
    all_gather x1, waiting for transfers between devices, per_device(): lax.all_gather(jnp.stack((key_here, value_here)), 'ctx', axis=1, tiled=True)  26.2 us
    unnamed x10, local copies, waits for them, and re-layouts  11.5 us
    all_to_all x1, blocking collectives, per_device(): lax.all_to_all(values, 'head', split_axis=1, concat_axis=0, tiled=True)  11.3 us
    all_to_all x1, waiting for transfers between devices, per_device(): lax.all_to_all(grad_out, 'head', split_axis=1, concat_axis=0, tiled=True)  10.4 us
    slice x8, local copies, waits for them, and re-layouts, backward_block(): add_query, add_key, add_value = tile_grads(part[0], part[1], first_row)  10.2 us
    slice x8, local copies, waits for them, and re-layouts, forward_block(): return fold_keys(running, (part[0], part[1]), first_row)  10.2 us
  transfers between devices with their start and end apart: 10, of which 8 were waited for; matrix products, arithmetic and copies ran while one was open for 2% of the time, Pallas kernels for 0%

commit v1 on v0

--- a/solution.py
+++ b/solution.py
@@ -103,7 +103,12 @@
         jnp.full((local_heads, row_count), masked_low, jnp.float32),
         jnp.zeros((local_heads, row_count), jnp.float32),
     )
-    gathered = lax.all_gather(jnp.stack((key_here, value_here)), "ctx", axis=1, tiled=True)
+    gathered = jnp.concatenate(
+        lax.all_to_all(
+            jnp.stack([jnp.stack((key_here, value_here))] * lax.axis_size("ctx")), "ctx", 0, 0
+        ),
+        axis=1,
+    )
     span = row_count * math.gcd(cycle_size, max(1, 512 // row_count))
     block_total = cycle_size * row_count // span
 

time: 352 us -> 469 us (1.33)
  waiting for transfers between devices: 178 us -> 285 us
  local copies, waits for them, and re-layouts: 55.3 us -> 72.4 us
  blocking collectives: 11.3 us -> 0 us
    all_to_all x0 -> x2, waiting for transfers between devices: none -> 131 us  [the longest x1 123 us: per_device(): lax.all_to_all(jnp.stack([jnp.stack((key_here, value_here))] * lax.axis_s...]
    all_gather x1 -> x0, waiting for transfers between devices: 26.2 us -> none  [per_device(): lax.all_gather(jnp.stack((key_here, value_here)), 'ctx', axis=1, tiled=True)]
    all_to_all x0 -> x1, local copies, waits for them, and re-layouts: none -> 11.9 us  [per_device(): lax.all_to_all(jnp.stack([jnp.stack((key_here, value_here))] * lax.axis_s...]
    all_to_all x1 -> x0, blocking collectives: 11.3 us -> none  [per_device(): lax.all_to_all(values, 'head', split_axis=1, concat_axis=0, tiled=True)]
    all_to_all x0 -> x2, starting transfers between devices: none -> 8.91 us  [the longest x1 5.5 us: per_device(): lax.all_to_all(jnp.stack([jnp.stack((key_here, value_here))] * lax.axis_s...]
    reduce_scatter x1, waiting for transfers between devices: 50 us -> 55.9 us  [per_device(): lax.psum_scatter(key_sums[0].astype(jnp.bfloat16), 'ctx', scatter_dimensi...]
  transfers between devices with their start and end apart: 10 -> 11, of which waited for: 8 -> 9; matrix products, arithmetic and copies ran while one was open for 2% -> 2% of each run, Pallas kernels for 0% -> 0%
where the time goes in v1:
time: 469 us; the launch traced here: 467 us
  waiting for transfers between devices  285 us (61%)
  local copies, waits for them, and re-layouts  72.4 us (15%)
  starting transfers between devices  42 us (9%)
  matrix products  29.8 us (6%)
  other arithmetic  22.4 us (5%)
  between operations  14.3 us (3%)
    all_to_all x1, waiting for transfers between devices, per_device(): lax.all_to_all(jnp.stack([jnp.stack((key_here, value_here))] * lax.axis_s...  123 us
    reduce_scatter x1, waiting for transfers between devices, per_device(): lax.psum_scatter(key_sums[1].astype(jnp.bfloat16), 'ctx', scatter_dimensi...  60 us
    reduce_scatter x1, waiting for transfers between devices, per_device(): lax.psum_scatter(key_sums[0].astype(jnp.bfloat16), 'ctx', scatter_dimensi...  55.9 us
    all_to_all x1, local copies, waits for them, and re-layouts, per_device(): lax.all_to_all(jnp.stack([jnp.stack((key_here, value_here))] * lax.axis_s...  11.9 us
    unnamed x10, local copies, waits for them, and re-layouts  11.6 us
    slice x8, local copies, waits for them, and re-layouts, backward_block(): add_query, add_key, add_value = tile_grads(part[0], part[1], first_row)  10.2 us
    slice x8, local copies, waits for them, and re-layouts, forward_block(): return fold_keys(running, (part[0], part[1]), first_row)  10.2 us
    dynamic_update_slice x8, other arithmetic, backward_block(): lax.dynamic_update_slice_in_dim(key_sums, jnp.stack((add_key, add_value))...  9.38 us
  transfers between devices with their start and end apart: 11, of which 9 were waited for; matrix products, arithmetic and copies ran while one was open for 2% of the time, Pallas kernels for 0%

profile of v1, /device:TPU:0, one launch (start us, length us, event | category | flops | bytes accessed | tf_op | source)
XLA Modules:
  0.0 467.0 jit_solution(15217793196948300683)
XLA Ops:
  7.2 1.7 copy.146
  8.9 7.0 %all-to-all-start.3 = ((bf16[32,8,512]{2,0,1:T(8,128)(2,1)}), bf16[32,8,512]{2,0,1:T(8,128)(2,1)S(1)}, u32[]{:S(2)}, u32[]{:S(2)}) async-start(bf16[32,8,512]{2,0,1:T(8,128)(2,1)} %bitcast.95), calls=%async_computation.3 | async-start | bytes 524288 | tf_op jit(solution)/shard_map/all_to_all | solution.py:79
  16.0 1.7 copy.148
  17.6 7.1 %all-to-all-done.3 = bf16[32,8,512]{2,0,1:T(8,128)(2,1)S(1)} async-done(((bf16[32,8,512]{2,0,1:T(8,128)(2,1)}), bf16[32,8,512]{2,0,1:T(8,128)(2,1)S(1)}, u32[]{:S(2)}, u32[]{:S(2)}) %all-to-all-start.3) | async-done | bytes 262176 | tf_op jit(solution)/shard_map/all_to_all | solution.py:79
  24.7 3.4 all-to-all-start
  28.8 7.9 %all-to-all-done = bf16[32,8,512]{2,0,1:T(8,128)(2,1)S(1)} async-done(((bf16[32,8,512]{2,0,1:T(8,128)(2,1)}), bf16[32,8,512]{2,0,1:T(8,128)(2,1)S(1)}, u32[]{:S(2)}, u32[]{:S(2)}) %all-to-all-start) | async-done | bytes 262176 | tf_op jit(solution)/shard_map/all_to_all | solution.py:80
  36.8 3.4 all-to-all-start.1
  40.9 7.9 %all-to-all-done.1 = bf16[32,8,512]{2,0,1:T(8,128)(2,1)S(1)} async-done(((bf16[32,8,512]{2,0,1:T(8,128)(2,1)}), bf16[32,8,512]{2,0,1:T(8,128)(2,1)S(1)}, u32[]{:S(2)}, u32[]{:S(2)}) %all-to-all-start.1) | async-done | bytes 262176 | tf_op jit(solution)/shard_map/all_to_all | solution.py:81
  48.9 3.4 all-to-all-start.5
  52.5 8.4 %all-to-all-done.5 = bf16[32,8,512]{2,0,1:T(8,128)(2,1)S(1)} async-done(((bf16[32,8,512]{2,0,1:T(8,128)(2,1)}), bf16[32,8,512]{2,0,1:T(8,128)(2,1)S(1)}, u32[]{:S(2)}, u32[]{:S(2)}) %all-to-all-start.5) | async-done | bytes 262176 | tf_op jit(solution)/shard_map/all_to_all | solution.py:82
  60.9 4.2 stack.64
  65.1 5.5 %all-to-all-start.2 = ((bf16[16,2,256,512]{2,3,1,0:T(8,128)(2,1)}), bf16[16,2,256,512]{2,3,1,0:T(8,128)(2,1)}, u32[]{:S(2)}, u32[]{:S(2)}) async-start(bf16[16,2,256,512]{2,3,1,0:T(8,128)(2,1)} %stack.64), calls=%async_computation.2 | async-start | bytes 16777216 | tf_op jit(solution)/shard_map/all_to_all | solution.py:107
  70.9 123.0 %all-to-all-done.2 = bf16[16,2,256,512]{2,3,1,0:T(8,128)(2,1)} async-done(((bf16[16,2,256,512]{2,3,1,0:T(8,128)(2,1)}), bf16[16,2,256,512]{2,3,1,0:T(8,128)(2,1)}, u32[]{:S(2)}, u32[]{:S(2)}) %all-to-all-start.2) | async-done | bytes 8388640 | tf_op jit(solution)/shard_map/all_to_all | solution.py:107
  193.9 11.9 %copy.110 = bf16[16,2,256,512]{3,2,0,1:T(8,128)(2,1)} copy(bf16[16,2,256,512]{2,3,1,0:T(8,128)(2,1)} %all-to-all-done.2) | data formatting | bytes 16777216 | tf_op jit(solution)/shard_map/all_to_all | solution.py:107
  205.8 11.4 %copy.112 = bf16[2,4096,512]{1,2,0:T(8,128)(2,1)} copy(bf16[2,4096,512]{2,1,0:T(8,128)(2,1)} %bitcast.158) | data formatting | bytes 16777216
  217.3 29.7 %while.44 = (s32[]{:T(128)}, f32[256,4,128]{0,2,1:T(8,128)S(1)}, f32[4,256]{1,0:T(4,128)S(1)}, f32[4,256]{1,0:T(4,128)S(1)}, s32[32]{0:T(128)S(1)}, /*index=5*/b...) while((s32[]{:T(128)}, f32[256,4,128]{0,2,1:T(8,128)S(1)}, ...), condition=%wide.region_5.6_spmd.clone.clone.clone, body=%wide.region_0.5_spmd.clone.clone.clone.sunk | while | flops 276164096 | bytes 11359203 | solution.py:120
  217.8 1.3 constant_dynamic-slice_fusion.6
  221.5 1.3 constant_dynamic-slice_fusion.6
  225.2 1.3 constant_dynamic-slice_fusion.6
  228.9 1.3 constant_dynamic-slice_fusion.6
  232.6 1.3 constant_dynamic-slice_fusion.6
  236.4 1.3 constant_dynamic-slice_fusion.6
  240.1 1.3 constant_dynamic-slice_fusion.6
  243.8 1.3 constant_dynamic-slice_fusion.6
  248.1 4.3 broadcast_in_dim.271
  252.4 43.3 %while.45 = (s32[]{:T(128)}, f32[256,4,128]{0,2,1:T(8,128)S(1)}, bf16[2,4096,4,128]{3,1,2,0:T(8,128)(2,1)}, bf16[2,4096,512]{1,2,0:T(8,128)(2,1)}, s32[32]{0:T(1...) while((s32[]{:T(128)}, f32[256,4,128]{0,2,1:T(8,128)S(1)}, ...), condition=%wide.region_10.11_spmd.clone.clone.clone, body=%wide.region_7.10_spmd.clone.clone.clone.sunk | while | flops 678286848 | bytes 18641908 | solution.py:147
  252.9 1.3 constant_dynamic-slice_fusion.7
  258.3 1.3 constant_dynamic-slice_fusion.7
  262.1 1.2 maximum_dynamic-update-slice_fusion.2
  263.8 1.3 constant_dynamic-slice_fusion.7
  267.5 1.2 maximum_dynamic-update-slice_fusion.2
  269.2 1.3 constant_dynamic-slice_fusion.7
  272.9 1.2 maximum_dynamic-update-slice_fusion.2
  274.6 1.3 constant_dynamic-slice_fusion.7
  280.0 1.3 constant_dynamic-slice_fusion.7
  283.7 1.2 maximum_dynamic-update-slice_fusion.2
  285.4 1.3 constant_dynamic-slice_fusion.7
  289.1 1.2 maximum_dynamic-update-slice_fusion.2
  290.9 1.3 constant_dynamic-slice_fusion.7
  295.7 5.7 %slice_bitcast_fusion = (bf16[4096,4,128]{2,0,1:T(8,128)(2,1)}, bf16[4096,4,128]{2,0,1:T(8,128)(2,1)}) fusion(bf16[2,4096,4,128]{3,1,2,0:T(8,128)(2,1)} %get-tuple-element.567), kind=kLoop, calls=%fused_computation.121 | loop fusion | bytes 16777216 | tf_op jit(solution)/shard_map/convert_element_type | solution.py:153
  303.0 3.4 all-to-all-start.4
  307.5 7.7 %all-to-all-done.4 = bf16[8,32,512]{2,1,0:T(8,128)(2,1)S(1)} async-done(((bf16[8,32,512]{2,1,0:T(8,128)(2,1)}), bf16[8,32,512]{2,1,0:T(8,128)(2,1)S(1)}, u32[]{:S(2)}, u32[]{:S(2)}) %all-to-all-start.4) | async-done | bytes 262176 | tf_op jit(solution)/shard_map/all_to_all | solution.py:161
  315.2 3.4 all-to-all-start.6
  318.6 55.9 %reduce-scatter.3.cloned.1.call-done = bf16[256,4,128]{2,0,1:T(8,128)(2,1)} async-done(((bf16[4096,4,128]{2,0,1:T(8,128)(2,1)}), bf16[256,4,128]{2,0,1:T(8,128)(2,1)}) %reduce-scatter.3.cloned.1.call-update) | async-done | bytes 262160 | tf_op jit(solution)/shard_map/reduce_scatter | solution.py:149
  376.5 5.9 %all-to-all-start.7 = ((bf16[8,32,512]{2,1,0:T(8,128)(2,1)}), bf16[8,32,512]{2,1,0:T(8,128)(2,1)S(1)}, u32[]{:S(2)}, u32[]{:S(2)}) async-start(bf16[8,32,512]{2,1,0:T(8,128)(2,1)} %all_to_all.128), calls=%async_computation.8 | async-start | bytes 524288 | tf_op jit(solution)/shard_map/all_to_all | solution.py:163
  382.4 60.0 %reduce-scatter.5.cloned.1.call-done = bf16[256,4,128]{2,0,1:T(8,128)(2,1)} async-done(((bf16[4096,4,128]{2,0,1:T(8,128)(2,1)}), bf16[256,4,128]{2,0,1:T(8,128)(2,1)}) %reduce-scatter.5.cloned.1.call-update) | async-done | bytes 262160 | tf_op jit(solution)/shard_map/reduce_scatter | solution.py:152
  444.3 6.4 %all-to-all-start.8 = ((bf16[8,32,512]{2,1,0:T(8,128)(2,1)}), bf16[8,32,512]{2,1,0:T(8,128)(2,1)S(1)}, u32[]{:S(2)}, u32[]{:S(2)}) async-start(bf16[8,32,512]{2,1,0:T(8,128)(2,1)} %all_to_all.132), calls=%async_computation.10 | async-start | bytes 524288 | tf_op jit(solution)/shard_map/all_to_all | solution.py:164
  452.9 6.6 %all-to-all-done.8 = bf16[8,32,512]{2,1,0:T(8,128)(2,1)S(1)} async-done(((bf16[8,32,512]{2,1,0:T(8,128)(2,1)}), bf16[8,32,512]{2,1,0:T(8,128)(2,1)S(1)}, u32[]{:S(2)}, u32[]{:S(2)}) %all-to-all-start.8) | async-done | bytes 262176 | tf_op jit(solution)/shard_map/all_to_all | solution.py:164
  (244 shorter events, 58.1 us)
Async XLA Ops:
  7.2 20.9 %copy-start = (bf16[32,4096]{1,0:T(8,128)(2,1)S(1)}, bf16[32,4096]{1,0:T(8,128)(2,1)}, u32[]{:S(2)}) copy-start(bf16[32,4096]{1,0:T(8,128)(2,1)} %param.11) | copy-start | bytes 786436
  7.2 33.0 %copy-start.1 = (bf16[32,4096]{1,0:T(8,128)(2,1)S(1)}, bf16[32,4096]{1,0:T(8,128)(2,1)}, u32[]{:S(2)}) copy-start(bf16[32,4096]{1,0:T(8,128)(2,1)} %param.12) | copy-start | bytes 786436
  8.9 15.8 %all-to-all-start.3 = ((bf16[32,8,512]{2,0,1:T(8,128)(2,1)}), bf16[32,8,512]{2,0,1:T(8,128)(2,1)S(1)}, u32[]{:S(2)}, u32[]{:S(2)}) async-start(bf16[32,8,512]{2,0,1:T(8,128)(2,1)} %bitcast.95), calls=%async_computation.3 | async-start | bytes 524288 | tf_op jit(solution)/shard_map/all_to_all | solution.py:79
  24.7 12.1 %all-to-all-start = ((bf16[32,8,512]{2,0,1:T(8,128)(2,1)}), bf16[32,8,512]{2,0,1:T(8,128)(2,1)S(1)}, u32[]{:S(2)}, u32[]{:S(2)}) async-start(bf16[32,8,512]{2,0,1:T(8,128)(2,1)} %bitcast.97), calls=%async_computation | async-start | bytes 524288 | tf_op jit(solution)/shard_map/all_to_all | solution.py:80
  36.8 12.1 %all-to-all-start.1 = ((bf16[32,8,512]{2,0,1:T(8,128)(2,1)}), bf16[32,8,512]{2,0,1:T(8,128)(2,1)S(1)}, u32[]{:S(2)}, u32[]{:S(2)}) async-start(bf16[32,8,512]{2,0,1:T(8,128)(2,1)} %bitcast.96), calls=%async_computation.1 | async-start | bytes 524288 | tf_op jit(solution)/shard_map/all_to_all | solution.py:81
  48.9 12.1 %all-to-all-start.5 = ((bf16[32,8,512]{2,0,1:T(8,128)(2,1)}), bf16[32,8,512]{2,0,1:T(8,128)(2,1)S(1)}, u32[]{:S(2)}, u32[]{:S(2)}) async-start(bf16[32,8,512]{2,0,1:T(8,128)(2,1)} %bitcast.94), calls=%async_computation.5 | async-start | bytes 524288 | tf_op jit(solution)/shard_map/all_to_all | solution.py:82
  65.1 128.8 %all-to-all-start.2 = ((bf16[16,2,256,512]{2,3,1,0:T(8,128)(2,1)}), bf16[16,2,256,512]{2,3,1,0:T(8,128)(2,1)}, u32[]{:S(2)}, u32[]{:S(2)}) async-start(bf16[16,2,256,512]{2,3,1,0:T(8,128)(2,1)} %stack.64), calls=%async_computation.2 | async-start | bytes 16777216 | tf_op jit(solution)/shard_map/all_to_all | solution.py:107
  70.6 303.9 %reduce-scatter.3.cloned.1.call-start = ((), (), s32[]{:S(2)}) async-start(), calls=%async_computation.11 | async-start | bytes 4456448 | tf_op jit(solution)/shard_map/reduce_scatter | solution.py:149
  205.8 11.4 %copy-start.2 = (s32[32]{0:T(128)S(1)}, s32[32]{0:T(128)}, u32[]{:S(2)}) copy-start(s32[32]{0:T(128)} %param.13) | copy-start | bytes 388
  301.5 140.9 %reduce-scatter.5.cloned.1.call-start = ((), (), s32[]{:S(2)}) async-start(), calls=%async_computation.12 | async-start | bytes 4456448 | tf_op jit(solution)/shard_map/reduce_scatter | solution.py:152
  303.0 12.2 %all-to-all-start.4 = ((bf16[8,32,512]{2,1,0:T(8,128)(2,1)}), bf16[8,32,512]{2,1,0:T(8,128)(2,1)S(1)}, u32[]{:S(2)}, u32[]{:S(2)}) async-start(bf16[8,32,512]{2,1,0:T(8,128)(2,1)} %all_to_all.117), calls=%async_computation.4 | async-start | bytes 524288 | tf_op jit(solution)/shard_map/all_to_all | solution.py:161
  315.2 61.2 %all-to-all-start.6 = ((bf16[8,32,512]{2,1,0:T(8,128)(2,1)}), bf16[8,32,512]{2,1,0:T(8,128)(2,1)S(1)}, u32[]{:S(2)}, u32[]{:S(2)}) async-start(bf16[8,32,512]{2,1,0:T(8,128)(2,1)} %all_to_all.124), calls=%async_computation.6 | async-start | bytes 524288 | tf_op jit(solution)/shard_map/all_to_all | solution.py:162
  376.5 67.8 %all-to-all-start.7 = ((bf16[8,32,512]{2,1,0:T(8,128)(2,1)}), bf16[8,32,512]{2,1,0:T(8,128)(2,1)S(1)}, u32[]{:S(2)}, u32[]{:S(2)}) async-start(bf16[8,32,512]{2,1,0:T(8,128)(2,1)} %all_to_all.128), calls=%async_computation.8 | async-start | bytes 524288 | tf_op jit(solution)/shard_map/all_to_all | solution.py:163
  444.3 15.1 %all-to-all-start.8 = ((bf16[8,32,512]{2,1,0:T(8,128)(2,1)}), bf16[8,32,512]{2,1,0:T(8,128)(2,1)S(1)}, u32[]{:S(2)}, u32[]{:S(2)}) async-start(bf16[8,32,512]{2,1,0:T(8,128)(2,1)} %all_to_all.132), calls=%async_computation.10 | async-start | bytes 524288 | tf_op jit(solution)/shard_map/all_to_all | solution.py:164
Sparse Core Ops, SparseCore 0:
  301.6 72.8 reduce-scatter.2
  376.9 65.3 reduce-scatter.4
